TPU v7x, 256 devices: a whole 4x4x8 slice. The times are simulated.
256 devices in a mesh: slab: 32 (over x, y, core), orb: 8 (over z).
Axes of the slice: x: 4, y: 4, z: 8, core: 2. Of those that a mesh axis runs over, the one named last changes fastest.
Arguments:
- orbitals: float32 [256, 65536], P('orb', 'slab'), may hold values from -6 to 6
- cell_matrices: bfloat16 [256, 512, 512], P('slab'), as said below
- connectivity: int32 [256, 512], P('slab'), may hold values from 0 to 2559, as said below
- face_lower: int32 [8192], P('slab'), may hold values from 0 to 2047, as said below
- face_upper: int32 [8192], P('slab'), may hold values from 0 to 2047, as said below
Outputs:
- orthonormal_orbitals: float32 [256, 65536], P('orb', 'slab')
Inputs may be any that keep to these rules, and one draw needn't show every extreme that they name: `connectivity`: each row names 512 distinct positions of its slab's extended numbering. `face_lower`: each slab's block of 256 entries names distinct own nodes; it shares no entry with the same slab's block of face_upper. `face_upper`: each slab's block of 256 entries names distinct own nodes; it shares no entry with the same slab's block of face_lower. `cell_matrices`: each cell matrix is symmetric.
All inputs are finite; a program needn't handle non-finite values.
Results may differ from a plain program's by a relative error of at most 0.023.
Values may be sent and summed in bfloat16 or wider, within the bound.
A program may use at most 64 MiB of HBM per device.

v0:
```python
import math
import jax
import jax.numpy as jnp
from jax import lax
from jax.sharding import PartitionSpec as P

CELL_NODES = 512
DEGREE = 4
FACE = 256


def extended_2(cells, sides, width):
    for axis, dim in sides:
        count = lax.axis_size(axis)
        ends = count - 1
        head = lax.slice_in_dim(cells, 0, width, axis=dim)
        tail = lax.slice_in_dim(cells, cells.shape[dim] - width, cells.shape[dim], axis=dim)
        cells = jnp.concatenate(
            [
                lax.ppermute(tail, axis, [(i, (i + 1) % count) for i in range(ends)]),
                cells,
                lax.ppermute(head, axis, [((i + 1) % count, i) for i in range(ends)]),
            ],
            axis=dim,
        )
    return cells


def partner_2(value, axis, distance):
    mask = 2**distance
    pairs = [(source, source ^ mask) for source in range(lax.axis_size(axis))]
    return lax.ppermute(value, axis, pairs)


def gram_of(matrix):
    return lax.dot_general(
        matrix,
        matrix,
        (((1,), (1,)), ((), ())),
        precision=lax.Precision.HIGHEST,
        preferred_element_type=jnp.float32,
    )


def forward_solve(factor, values):
    return lax.linalg.triangular_solve(factor, values, left_side=True, lower=True)


def three_parts(values):
    upper_part = values.astype(jnp.bfloat16)
    remain = values - upper_part.astype(jnp.float32)
    middle_part = remain.astype(jnp.bfloat16)
    lowest_part = (remain - middle_part.astype(jnp.float32)).astype(jnp.bfloat16)
    return jnp.concatenate([upper_part, middle_part, lowest_part], axis=0)


def spread_back(values, table):
    row_count = values.shape[0]
    stacked = lax.dot_general(
        three_parts(values), table, (((1,), (1,)), ((), ())), preferred_element_type=jnp.float32
    )
    return stacked[:row_count] + stacked[row_count : 2 * row_count] + stacked[2 * row_count :]


def apply_cells(wave_field, cell_matrices, connectivity, face_table):
    rounded = wave_field.astype(jnp.bfloat16)
    orb_count, node_count = rounded.shape
    face_rows = jnp.dot(rounded, face_table, preferred_element_type=jnp.float32).astype(
        jnp.bfloat16
    )
    bordered = extended_2(face_rows, (("slab", 1),), FACE)
    extended = jnp.concatenate([bordered[:, :FACE], rounded, bordered[:, 3 * FACE :]], axis=1)
    ext_count = extended.shape[1]
    positions = lax.broadcasted_iota(jnp.int32, (ext_count, CELL_NODES), 0)

    def add_cell(summed, inputs):
        cell_block, cell_row = inputs
        picker = (positions == cell_row[None, :]).astype(jnp.bfloat16)
        pieces = jnp.dot(extended, picker, preferred_element_type=jnp.float32).astype(jnp.bfloat16)
        cell_terms = jnp.dot(pieces, cell_block, preferred_element_type=jnp.float32)
        return (summed + spread_back(cell_terms, picker), None)

    summed, _ = lax.scan(
        add_cell, jnp.zeros((orb_count, ext_count), jnp.float32), (cell_matrices, connectivity)
    )
    returned = jnp.concatenate([summed[:, :FACE], summed[:, FACE + node_count :]], axis=1)
    received = extended_2(returned, (("slab", 1),), FACE)
    incoming = jnp.concatenate([received[:, :FACE], received[:, 3 * FACE :]], axis=1)
    return summed[:, FACE : FACE + node_count] + spread_back(incoming, face_table)


def per_device(orbitals, cell_matrices, connectivity, face_lower, face_upper):
    node_count = orbitals.shape[1]
    face_nodes = jnp.concatenate([face_lower, face_upper], axis=0)
    face_table = (
        lax.broadcasted_iota(jnp.int32, (node_count, face_nodes.shape[0]), 0) == face_nodes[None, :]
    ).astype(jnp.bfloat16)
    previous = orbitals
    current = apply_cells(orbitals, cell_matrices, connectivity, face_table)
    for degree_step in range(1, DEGREE):
        following = 2.0 * apply_cells(current, cell_matrices, connectivity, face_table) - previous
        previous, current = (current, following)
    block_rows = orbitals.shape[0]
    norm_scale = math.sqrt(orbitals.shape[1] * lax.axis_size("slab"))
    gathered = lax.all_gather(current.astype(jnp.bfloat16), "orb", axis=0, tiled=True).astype(
        current.dtype
    )
    factor = jnp.linalg.cholesky(gram_of(gathered))
    for level in range(lax.axis_size("slab").bit_length() - 1):
        partner = partner_2(factor.astype(jnp.bfloat16), "slab", level).astype(factor.dtype)
        factor = jnp.linalg.cholesky(gram_of(factor) + gram_of(partner))
    solved = forward_solve(factor, gathered) * norm_scale
    result = lax.dynamic_slice_in_dim(solved, lax.axis_index("orb") * block_rows, block_rows, 0)
    return result


def solution(mesh):
    in_specs = (P("orb", "slab"), P("slab", None, None), P("slab", None), P("slab"), P("slab"))
    out_specs = P("orb", "slab")
    return jax.shard_map(
        per_device, mesh=mesh, in_specs=in_specs, out_specs=out_specs, check_vma=False
    )
```

profile of v0, /device:TPU:2, one launch (start us, length us, event | category | flops | bytes accessed | tf_op | source)
XLA Modules:
  0.0 538.3 jit_solution(7230007769574144148)
XLA Ops:
  18.1 33.1 %while.46 = (s32[]{:T(128)}, f32[32,2560]{1,0:T(8,128)S(1)}, s32[8,512]{1,0:T(8,128)}, bf16[32,2560]{1,0:T(8,128)(2,1)S(1)}, bf16[8,512,512]{2,1,0:T(8,128)(2,1)}, /*index=5*/s32[]{:T(128)}, s32[]{:T(128)}) while((s32[]{:T(128)}, f32[32,2560]{1,0:T(8,128)S(1)}, s32[8,512]{1,0:T(8,128)}, bf16[32,2560]{1,0:T(8,128)(2,1)S(1)}, ...), condition=%wide.region_1.2_spmd.clone, body=%wide.region_0.1_spmd.clone.sunk | while | flops 357007360 | bytes 3514971 | solution.py:83
  71.5 27.5 %while.47 = (s32[]{:T(128)}, f32[32,2560]{1,0:T(8,128)S(1)}, s32[8,512]{1,0:T(8,128)S(1)}, bf16[32,2560]{1,0:T(8,128)(2,1)S(1)}, bf16[8,512,512]{2,1,0:T(8,128)(2,1)}, /*index=5*/s32[]{:T(128)}, s32[]{:T(128)}) while((s32[]{:T(128)}, f32[32,2560]{1,0:T(8,128)S(1)}, s32[8,512]{1,0:T(8,128)S(1)}, bf16[32,2560]{1,0:T(8,128)(2,1)S(1)}, ...), condition=%wide.region_3.4_spmd.clone, body=%wide.region_2.3_spmd.clone.sunk | while | flops 357007360 | bytes 3514971 | solution.py:83
  119.3 27.5 %while.48 = (s32[]{:T(128)}, f32[32,2560]{1,0:T(8,128)S(1)}, s32[8,512]{1,0:T(8,128)S(1)}, bf16[32,2560]{1,0:T(8,128)(2,1)S(1)}, bf16[8,512,512]{2,1,0:T(8,128)(2,1)}, /*index=5*/s32[]{:T(128)}, s32[]{:T(128)}) while((s32[]{:T(128)}, f32[32,2560]{1,0:T(8,128)S(1)}, s32[8,512]{1,0:T(8,128)S(1)}, bf16[32,2560]{1,0:T(8,128)(2,1)S(1)}, ...), condition=%wide.region_5.6_spmd.clone, body=%wide.region_4.5_spmd.clone.sunk | while | flops 357007360 | bytes 3514971 | solution.py:83
  167.0 27.5 %while.49 = (s32[]{:T(128)}, f32[32,2560]{1,0:T(8,128)S(1)}, s32[8,512]{1,0:T(8,128)S(1)}, bf16[32,2560]{1,0:T(8,128)(2,1)S(1)}, bf16[8,512,512]{2,1,0:T(8,128)(2,1)}, /*index=5*/s32[]{:T(128)}, s32[]{:T(128)}) while((s32[]{:T(128)}, f32[32,2560]{1,0:T(8,128)S(1)}, s32[8,512]{1,0:T(8,128)S(1)}, bf16[32,2560]{1,0:T(8,128)(2,1)S(1)}, ...), condition=%wide.region_7.8_spmd.clone, body=%wide.region_6.7_spmd.clone.sunk | while | flops 357007360 | bytes 3514971 | solution.py:83
  205.5 41.9 %all-gather.2.cloned.1.call-done = bf16[256,2048]{1,0:T(8,128)(2,1)} async-done(((bf16[32,2048]{1,0:T(8,128)(2,1)}), bf16[256,2048]{1,0:T(8,128)(2,1)}) %all-gather.2.cloned.1.call-update) | async-done | bytes 1048592 | tf_op jit(solution)/shard_map/all_gather | solution.py:105
  249.7 11.7 %cholesky.298 = f32[128,128]{1,0:T(8,128)S(1)} custom-call(f32[128,128]{1,0:T(8,128)S(1)} %cholesky.498), custom_call_target="Cholesky" | custom-call | tf_op jit(solution)/shard_map/jit(cholesky)/cholesky | solution.py:108
  261.4 9.8 %custom-call.21 = f32[1,128,128]{1,2,0:T(8,128)S(1)} custom-call(f32[1,128,128]{2,1,0:T(8,128)S(1)} %get-tuple-element.323), custom_call_target="InvertDiagBlocksLowerTriangular" | custom-call | tf_op jit(solution)/shard_map/jit(cholesky)/cholesky | solution.py:108
  271.7 11.7 %cholesky.315 = f32[128,128]{1,0:T(8,128)S(1)} custom-call(f32[128,128]{1,0:T(8,128)S(1)} %convolution_subtract_fusion.1), custom_call_target="Cholesky" | custom-call | tf_op jit(solution)/shard_map/jit(cholesky)/cholesky | solution.py:108
  295.5 11.7 %cholesky.332 = f32[128,128]{1,0:T(8,128)S(1)} custom-call(f32[128,128]{1,0:T(8,128)S(1)} %cholesky.501), custom_call_target="Cholesky" | custom-call | tf_op jit(solution)/shard_map/jit(cholesky)/cholesky | solution.py:111
  307.3 9.8 %custom-call.22 = f32[1,128,128]{1,2,0:T(8,128)S(1)} custom-call(f32[1,128,128]{2,1,0:T(8,128)S(1)} %get-tuple-element.319), custom_call_target="InvertDiagBlocksLowerTriangular" | custom-call | tf_op jit(solution)/shard_map/jit(cholesky)/cholesky | solution.py:111
  317.6 11.7 %cholesky.349 = f32[128,128]{1,0:T(8,128)S(1)} custom-call(f32[128,128]{1,0:T(8,128)S(1)} %slice_subtract_fusion.4), custom_call_target="Cholesky" | custom-call | tf_op jit(solution)/shard_map/jit(cholesky)/cholesky | solution.py:111
  338.1 11.7 %cholesky.366 = f32[128,128]{1,0:T(8,128)S(1)} custom-call(f32[128,128]{1,0:T(8,128)S(1)} %cholesky.504), custom_call_target="Cholesky" | custom-call | tf_op jit(solution)/shard_map/jit(cholesky)/cholesky | solution.py:111
  349.9 9.8 %custom-call.23 = f32[1,128,128]{1,2,0:T(8,128)S(1)} custom-call(f32[1,128,128]{2,1,0:T(8,128)S(1)} %get-tuple-element.315), custom_call_target="InvertDiagBlocksLowerTriangular" | custom-call | tf_op jit(solution)/shard_map/jit(cholesky)/cholesky | solution.py:111
  360.2 11.7 %cholesky.383 = f32[128,128]{1,0:T(8,128)S(1)} custom-call(f32[128,128]{1,0:T(8,128)S(1)} %slice_subtract_fusion.3), custom_call_target="Cholesky" | custom-call | tf_op jit(solution)/shard_map/jit(cholesky)/cholesky | solution.py:111
  381.8 11.7 %cholesky.400 = f32[128,128]{1,0:T(8,128)S(1)} custom-call(f32[128,128]{1,0:T(8,128)S(1)} %cholesky.507), custom_call_target="Cholesky" | custom-call | tf_op jit(solution)/shard_map/jit(cholesky)/cholesky | solution.py:111
  393.6 9.8 %custom-call.24 = f32[1,128,128]{1,2,0:T(8,128)S(1)} custom-call(f32[1,128,128]{2,1,0:T(8,128)S(1)} %get-tuple-element.311), custom_call_target="InvertDiagBlocksLowerTriangular" | custom-call | tf_op jit(solution)/shard_map/jit(cholesky)/cholesky | solution.py:111
  403.9 11.7 %cholesky.417 = f32[128,128]{1,0:T(8,128)S(1)} custom-call(f32[128,128]{1,0:T(8,128)S(1)} %slice_subtract_fusion.2), custom_call_target="Cholesky" | custom-call | tf_op jit(solution)/shard_map/jit(cholesky)/cholesky | solution.py:111
  423.8 11.7 %cholesky.434 = f32[128,128]{1,0:T(8,128)S(1)} custom-call(f32[128,128]{1,0:T(8,128)S(1)} %cholesky.510), custom_call_target="Cholesky" | custom-call | tf_op jit(solution)/shard_map/jit(cholesky)/cholesky | solution.py:111
  435.6 9.8 %custom-call.25 = f32[1,128,128]{1,2,0:T(8,128)S(1)} custom-call(f32[1,128,128]{2,1,0:T(8,128)S(1)} %get-tuple-element.307), custom_call_target="InvertDiagBlocksLowerTriangular" | custom-call | tf_op jit(solution)/shard_map/jit(cholesky)/cholesky | solution.py:111
  445.9 11.7 %cholesky.451 = f32[128,128]{1,0:T(8,128)S(1)} custom-call(f32[128,128]{1,0:T(8,128)S(1)} %slice_subtract_fusion.1), custom_call_target="Cholesky" | custom-call | tf_op jit(solution)/shard_map/jit(cholesky)/cholesky | solution.py:111
  467.4 11.7 %cholesky.468 = f32[128,128]{1,0:T(8,128)S(1)} custom-call(f32[128,128]{1,0:T(8,128)S(1)} %cholesky.513), custom_call_target="Cholesky" | custom-call | tf_op jit(solution)/shard_map/jit(cholesky)/cholesky | solution.py:111
  479.1 9.8 %custom-call.26 = f32[1,128,128]{1,2,0:T(8,128)S(1)} custom-call(f32[1,128,128]{2,1,0:T(8,128)S(1)} %get-tuple-element.303), custom_call_target="InvertDiagBlocksLowerTriangular" | custom-call | tf_op jit(solution)/shard_map/jit(cholesky)/cholesky | solution.py:111
  489.4 11.7 %cholesky.485 = f32[128,128]{1,0:T(8,128)S(1)} custom-call(f32[128,128]{1,0:T(8,128)S(1)} %slice_subtract_fusion), custom_call_target="Cholesky" | custom-call | tf_op jit(solution)/shard_map/jit(cholesky)/cholesky | solution.py:111
  507.8 19.7 %custom-call.11 = f32[2,128,128]{1,2,0:T(8,128)S(1)} custom-call(f32[2,128,128]{2,1,0:T(8,128)S(1)} %get-tuple-element.145), custom_call_target="InvertDiagBlocksLowerTriangular" | custom-call | tf_op jit(solution)/shard_map/triangular_solve | solution.py:46
  (310 shorter events, 257.8 us)
Async XLA Ops:
  6.5 240.9 %all-gather.2.cloned.1.call-start = ((), (), s32[]{:S(2)}) async-start(), calls=%async_computation | async-start | bytes 1179648 | tf_op jit(solution)/shard_map/all_gather | solution.py:105
  9.0 7.7 %collective-permute-start = (bf16[32,256]{1,0:T(8,128)(2,1)S(1)}, bf16[32,256]{1,0:T(8,128)(2,1)S(1)}, u32[]{:S(2)}, u32[]{:S(2)}) collective-permute-start(bf16[32,256]{1,0:T(8,128)(2,1)S(1)} %get-tuple-element.342), channel_id=1, source_target_pairs={{0,8},{8,16},{16,24},{24,32},{32,40},{40,48},{48,56},{56,64},{64,7... | collective-permute-start | bytes 49160 | tf_op jit(solution)/shard_map/ppermute | solution.py:20
  10.9 7.2 %collective-permute-start.1 = (bf16[32,256]{1,0:T(8,128)(2,1)S(1)}, bf16[32,256]{1,0:T(8,128)(2,1)S(1)}, u32[]{:S(2)}, u32[]{:S(2)}) collective-permute-start(bf16[32,256]{1,0:T(8,128)(2,1)S(1)} %get-tuple-element.343), channel_id=1, source_target_pairs={{8,0},{16,8},{24,16},{32,24},{40,32},{48,40},{56,48},{64,56},{72,6... | collective-permute-start | bytes 49160 | tf_op jit(solution)/shard_map/ppermute | solution.py:22
  51.3 7.7 %collective-permute-start.2 = (f32[32,256]{1,0:T(8,128)S(1)}, f32[32,256]{1,0:T(8,128)S(1)}, u32[]{:S(2)}, u32[]{:S(2)}) collective-permute-start(f32[32,256]{1,0:T(8,128)S(1)} %get-tuple-element.299), channel_id=1, source_target_pairs={{0,8},{8,16},{16,24},{24,32},{32,40},{40,48},{48,56},{56,64},{64,7... | collective-permute-start | bytes 98312 | tf_op jit(solution)/shard_map/ppermute | solution.py:20
  53.2 7.3 %collective-permute-start.3 = (f32[32,256]{1,0:T(8,128)S(1)}, f32[32,256]{1,0:T(8,128)S(1)}, u32[]{:S(2)}, u32[]{:S(2)}) collective-permute-start(f32[32,256]{1,0:T(8,128)S(1)} %get-tuple-element.298), channel_id=1, source_target_pairs={{8,0},{16,8},{24,16},{32,24},{40,32},{48,40},{56,48},{64,56},{72,6... | collective-permute-start | bytes 98312 | tf_op jit(solution)/shard_map/ppermute | solution.py:22
  62.3 7.7 %collective-permute-start.4 = (bf16[32,256]{1,0:T(8,128)(2,1)S(1)}, bf16[32,256]{1,0:T(8,128)(2,1)S(1)}, u32[]{:S(2)}, u32[]{:S(2)}) collective-permute-start(bf16[32,256]{1,0:T(8,128)(2,1)S(1)} %get-tuple-element.340), channel_id=1, source_target_pairs={{0,8},{8,16},{16,24},{24,32},{32,40},{40,48},{48,56},{56,64},{64,7... | collective-permute-start | bytes 49160 | tf_op jit(solution)/shard_map/ppermute | solution.py:20
  64.3 7.2 %collective-permute-start.5 = (bf16[32,256]{1,0:T(8,128)(2,1)S(1)}, bf16[32,256]{1,0:T(8,128)(2,1)S(1)}, u32[]{:S(2)}, u32[]{:S(2)}) collective-permute-start(bf16[32,256]{1,0:T(8,128)(2,1)S(1)} %get-tuple-element.341), channel_id=1, source_target_pairs={{8,0},{16,8},{24,16},{32,24},{40,32},{48,40},{56,48},{64,56},{72,6... | collective-permute-start | bytes 49160 | tf_op jit(solution)/shard_map/ppermute | solution.py:22
  71.5 37.7 %copy-start.1 = (f32[32,2048]{1,0:T(8,128)S(1)}, f32[32,2048]{1,0:T(8,128)}, u32[]{:S(2)}) copy-start(f32[32,2048]{1,0:T(8,128)} %param.14) | copy-start | bytes 786436
  99.0 7.7 %collective-permute-start.6 = (f32[32,256]{1,0:T(8,128)S(1)}, f32[32,256]{1,0:T(8,128)S(1)}, u32[]{:S(2)}, u32[]{:S(2)}) collective-permute-start(f32[32,256]{1,0:T(8,128)S(1)} %get-tuple-element.297), channel_id=1, source_target_pairs={{0,8},{8,16},{16,24},{24,32},{32,40},{40,48},{48,56},{56,64},{64,7... | collective-permute-start | bytes 98312 | tf_op jit(solution)/shard_map/ppermute | solution.py:20
  101.0 7.3 %collective-permute-start.7 = (f32[32,256]{1,0:T(8,128)S(1)}, f32[32,256]{1,0:T(8,128)S(1)}, u32[]{:S(2)}, u32[]{:S(2)}) collective-permute-start(f32[32,256]{1,0:T(8,128)S(1)} %get-tuple-element.296), channel_id=1, source_target_pairs={{8,0},{16,8},{24,16},{32,24},{40,32},{48,40},{56,48},{64,56},{72,6... | collective-permute-start | bytes 98312 | tf_op jit(solution)/shard_map/ppermute | solution.py:22
  110.1 7.7 %collective-permute-start.8 = (bf16[32,256]{1,0:T(8,128)(2,1)S(1)}, bf16[32,256]{1,0:T(8,128)(2,1)S(1)}, u32[]{:S(2)}, u32[]{:S(2)}) collective-permute-start(bf16[32,256]{1,0:T(8,128)(2,1)S(1)} %get-tuple-element.338), channel_id=1, source_target_pairs={{0,8},{8,16},{16,24},{24,32},{32,40},{40,48},{48,56},{56,64},{64,7... | collective-permute-start | bytes 49160 | tf_op jit(solution)/shard_map/ppermute | solution.py:20
  112.1 7.2 %collective-permute-start.9 = (bf16[32,256]{1,0:T(8,128)(2,1)S(1)}, bf16[32,256]{1,0:T(8,128)(2,1)S(1)}, u32[]{:S(2)}, u32[]{:S(2)}) collective-permute-start(bf16[32,256]{1,0:T(8,128)(2,1)S(1)} %get-tuple-element.339), channel_id=1, source_target_pairs={{8,0},{16,8},{24,16},{32,24},{40,32},{48,40},{56,48},{64,56},{72,6... | collective-permute-start | bytes 49160 | tf_op jit(solution)/shard_map/ppermute | solution.py:22
  146.8 7.9 %collective-permute-start.10 = (f32[32,256]{1,0:T(8,128)S(1)}, f32[32,256]{1,0:T(8,128)S(1)}, u32[]{:S(2)}, u32[]{:S(2)}) collective-permute-start(f32[32,256]{1,0:T(8,128)S(1)} %get-tuple-element.295), channel_id=1, source_target_pairs={{0,8},{8,16},{16,24},{24,32},{32,40},{40,48},{48,56},{56,64},{64,7... | collective-permute-start | bytes 98312 | tf_op jit(solution)/shard_map/ppermute | solution.py:20
  148.7 7.3 %collective-permute-start.11 = (f32[32,256]{1,0:T(8,128)S(1)}, f32[32,256]{1,0:T(8,128)S(1)}, u32[]{:S(2)}, u32[]{:S(2)}) collective-permute-start(f32[32,256]{1,0:T(8,128)S(1)} %get-tuple-element.294), channel_id=1, source_target_pairs={{8,0},{16,8},{24,16},{32,24},{40,32},{48,40},{56,48},{64,56},{72,6... | collective-permute-start | bytes 98312 | tf_op jit(solution)/shard_map/ppermute | solution.py:22
  157.9 7.7 %collective-permute-start.12 = (bf16[32,256]{1,0:T(8,128)(2,1)S(1)}, bf16[32,256]{1,0:T(8,128)(2,1)S(1)}, u32[]{:S(2)}, u32[]{:S(2)}) collective-permute-start(bf16[32,256]{1,0:T(8,128)(2,1)S(1)} %get-tuple-element.336), channel_id=1, source_target_pairs={{0,8},{8,16},{16,24},{24,32},{32,40},{40,48},{48,56},{56,64},{64,7... | collective-permute-start | bytes 49160 | tf_op jit(solution)/shard_map/ppermute | solution.py:20
  159.8 7.2 %collective-permute-start.13 = (bf16[32,256]{1,0:T(8,128)(2,1)S(1)}, bf16[32,256]{1,0:T(8,128)(2,1)S(1)}, u32[]{:S(2)}, u32[]{:S(2)}) collective-permute-start(bf16[32,256]{1,0:T(8,128)(2,1)S(1)} %get-tuple-element.337), channel_id=1, source_target_pairs={{8,0},{16,8},{24,16},{32,24},{40,32},{48,40},{56,48},{64,56},{72,6... | collective-permute-start | bytes 49160 | tf_op jit(solution)/shard_map/ppermute | solution.py:22
  194.5 7.7 %collective-permute-start.14 = (f32[32,256]{1,0:T(8,128)S(1)}, f32[32,256]{1,0:T(8,128)S(1)}, u32[]{:S(2)}, u32[]{:S(2)}) collective-permute-start(f32[32,256]{1,0:T(8,128)S(1)} %get-tuple-element.293), channel_id=1, source_target_pairs={{0,8},{8,16},{16,24},{24,32},{32,40},{40,48},{48,56},{56,64},{64,7... | collective-permute-start | bytes 98312 | tf_op jit(solution)/shard_map/ppermute | solution.py:20
  196.4 7.3 %collective-permute-start.15 = (f32[32,256]{1,0:T(8,128)S(1)}, f32[32,256]{1,0:T(8,128)S(1)}, u32[]{:S(2)}, u32[]{:S(2)}) collective-permute-start(f32[32,256]{1,0:T(8,128)S(1)} %get-tuple-element.292), channel_id=1, source_target_pairs={{8,0},{16,8},{24,16},{32,24},{40,32},{48,40},{56,48},{64,56},{72,6... | collective-permute-start | bytes 98312 | tf_op jit(solution)/shard_map/ppermute | solution.py:22
  285.4 9.7 %collective-permute-start.16 = (bf16[256,256]{1,0:T(8,128)(2,1)S(1)}, bf16[256,256]{1,0:T(8,128)(2,1)S(1)}, u32[]{:S(2)}, u32[]{:S(2)}) collective-permute-start(bf16[256,256]{1,0:T(8,128)(2,1)S(1)} %fusion.143), channel_id=1, source_target_pairs={{0,8},{8,0},{16,24},{24,16},{32,40},{40,32},{48,56},{56,48},{64,72... | collective-permute-start | bytes 393224 | tf_op jit(solution)/shard_map/ppermute | solution.py:32
  331.8 5.8 %collective-permute-start.17 = (bf16[256,256]{1,0:T(8,128)(2,1)S(1)}, bf16[256,256]{1,0:T(8,128)(2,1)S(1)}, u32[]{:S(2)}, u32[]{:S(2)}) collective-permute-start(bf16[256,256]{1,0:T(8,128)(2,1)S(1)} %fusion.145), channel_id=1, source_target_pairs={{0,16},{8,24},{16,0},{24,8},{32,48},{40,56},{48,32},{56,40},{64,80... | collective-permute-start | bytes 393224 | tf_op jit(solution)/shard_map/ppermute | solution.py:32
  374.4 7.0 %collective-permute-start.18 = (bf16[256,256]{1,0:T(8,128)(2,1)S(1)}, bf16[256,256]{1,0:T(8,128)(2,1)S(1)}, u32[]{:S(2)}, u32[]{:S(2)}) collective-permute-start(bf16[256,256]{1,0:T(8,128)(2,1)S(1)} %fusion.147), channel_id=1, source_target_pairs={{0,32},{8,40},{16,48},{24,56},{32,0},{40,8},{48,16},{56,24},{64,96... | collective-permute-start | bytes 393224 | tf_op jit(solution)/shard_map/ppermute | solution.py:32
  418.2 5.2 collective-permute-start.19
  423.6 103.9 %copy-start = (bf16[256,2048]{1,0:T(8,128)(2,1)S(1)}, bf16[256,2048]{1,0:T(8,128)(2,1)}, u32[]{:S(2)}) copy-start(bf16[256,2048]{1,0:T(8,128)(2,1)} %all-gather.2.cloned.1.call-done) | copy-start | bytes 3145732
  460.2 6.8 %collective-permute-start.20 = (bf16[256,256]{1,0:T(8,128)(2,1)S(1)}, bf16[256,256]{1,0:T(8,128)(2,1)S(1)}, u32[]{:S(2)}, u32[]{:S(2)}) collective-permute-start(bf16[256,256]{1,0:T(8,128)(2,1)S(1)} %fusion.151), channel_id=1, source_target_pairs={{0,128},{8,136},{16,144},{24,152},{32,160},{40,168},{48,176},{56,1... | collective-permute-start | bytes 393224 | tf_op jit(solution)/shard_map/ppermute | solution.py:32
  (1 other events, 20.2 us)
Sparse Core Ops, SparseCore 0:
  205.6 41.7 all-gather.1
where the time goes:
time: 549 us; the launch traced here: 538 us
  other arithmetic  235 us (43%)
  matrix products  121 us (22%)
  starting transfers between devices  78.5 us (14%)
  waiting for transfers between devices  69.1 us (13%)
  between operations  22.1 us (4%)
  local copies, waits for them, and re-layouts  10.9 us (2%)
    another operation x35, other arithmetic, per_device(): factor = jnp.linalg.cholesky(gram_of(factor) + gram_of(partner))  173 us
    dot_general x32, matrix products, add_cell(): cell_terms = jnp.dot(pieces, cell_block, preferred_element_type=jnp.float32)  68.5 us
    ppermute x8, starting transfers between devices, extended_2(): lax.ppermute(head, axis, [((i + 1) % count, i) for i in range(ends)])  46.3 us
    all_gather x1, waiting for transfers between devices, per_device(): lax.all_gather(current.astype(jnp.bfloat16), 'orb', axis=0, tiled=True)  41.9 us
    dot_general x36, matrix products, spread_back(): lax.dot_general(three_parts(values), table, (((1,), (1,)), ((), ())), pre...  38.8 us
    another operation x6, other arithmetic, per_device(): factor = jnp.linalg.cholesky(gram_of(gathered))  33.9 us
    another operation x3, other arithmetic, forward_solve(): lax.linalg.triangular_solve(factor, values, left_side=True, lower=True)  19.7 us
    ppermute x5, starting transfers between devices, partner_2(): return lax.ppermute(value, axis, pairs)  16.8 us
  transfers between devices with their start and end apart: 22, of which 14 were waited for; matrix products, arithmetic and copies ran while one was open for 0% of the time, Pallas kernels for 0%

commit v1 on v0

--- a/solution.py
+++ b/solution.py
@@ -102,9 +102,12 @@
         previous, current = (current, following)
     block_rows = orbitals.shape[0]
     norm_scale = math.sqrt(orbitals.shape[1] * lax.axis_size("slab"))
-    gathered = lax.all_gather(current.astype(jnp.bfloat16), "orb", axis=0, tiled=True).astype(
-        current.dtype
-    )
+    gathered = jnp.concatenate(
+        lax.all_to_all(
+            jnp.stack([current.astype(jnp.bfloat16)] * lax.axis_size("orb")), "orb", 0, 0
+        ),
+        axis=0,
+    ).astype(current.dtype)
     factor = jnp.linalg.cholesky(gram_of(gathered))
     for level in range(lax.axis_size("slab").bit_length() - 1):
         partner = partner_2(factor.astype(jnp.bfloat16), "slab", level).astype(factor.dtype)

time: 549 us -> 529 us (0.964)
  the two profiles are of different devices: /device:TPU:2 before, /device:TPU:24 now
where the time goes in v1:
time: 529 us; the launch traced here: 518 us
  other arithmetic  235 us (44%)
  matrix products  120 us (23%)
  starting transfers between devices  81.7 us (15%)
  waiting for transfers between devices  59.6 us (11%)
  local copies, waits for them, and re-layouts  12.3 us (2%)
  between operations  8.91 us (2%)
    another operation x35, other arithmetic, per_device(): factor = jnp.linalg.cholesky(gram_of(factor) + gram_of(partner))  173 us
    dot_general x32, matrix products, add_cell(): cell_terms = jnp.dot(pieces, cell_block, preferred_element_type=jnp.float32)  68.5 us
    ppermute x8, starting transfers between devices, extended_2(): lax.ppermute(tail, axis, [(i, (i + 1) % count) for i in range(ends)])  41.7 us
    dot_general x36, matrix products, spread_back(): lax.dot_general(three_parts(values), table, (((1,), (1,)), ((), ())), pre...  38.8 us
    another operation x6, other arithmetic, per_device(): factor = jnp.linalg.cholesky(gram_of(gathered))  34 us
    all_to_all x1, waiting for transfers between devices, per_device(): lax.all_to_all(jnp.stack([current.astype(jnp.bfloat16)] * lax.axis_size('...  29.8 us
    another operation x3, other arithmetic, forward_solve(): lax.linalg.triangular_solve(factor, values, left_side=True, lower=True)  19.7 us
    ppermute x5, waiting for transfers between devices, partner_2(): return lax.ppermute(value, axis, pairs)  18.2 us
  transfers between devices with their start and end apart: 22, of which 14 were waited for; matrix products, arithmetic and copies ran while one was open for 0% of the time, Pallas kernels for 0%

profile of v1, /device:TPU:24, one launch (start us, length us, event | category | flops | bytes accessed | tf_op | source)
XLA Modules:
  0.0 518.5 jit_solution(1957067866903892398)
XLA Ops:
  9.5 33.1 %while.46 = (s32[]{:T(128)}, f32[32,2560]{1,0:T(8,128)S(1)}, s32[8,512]{1,0:T(8,128)}, bf16[32,2560]{1,0:T(8,128)(2,1)S(1)}, bf16[8,512,512]{2,1,0:T(8,128)(2,1)}, /*index=5*/s32[]{:T(128)}, s32[]{:T(128)}) while((s32[]{:T(128)}, f32[32,2560]{1,0:T(8,128)S(1)}, s32[8,512]{1,0:T(8,128)}, bf16[32,2560]{1,0:T(8,128)(2,1)S(1)}, ...), condition=%wide.region_1.2_spmd.clone, body=%wide.region_0.1_spmd.clone.sunk | while | flops 357007360 | bytes 3514971 | solution.py:83
  62.4 27.5 %while.47 = (s32[]{:T(128)}, f32[32,2560]{1,0:T(8,128)S(1)}, s32[8,512]{1,0:T(8,128)S(1)}, bf16[32,2560]{1,0:T(8,128)(2,1)S(1)}, bf16[8,512,512]{2,1,0:T(8,128)(2,1)}, /*index=5*/s32[]{:T(128)}, s32[]{:T(128)}) while((s32[]{:T(128)}, f32[32,2560]{1,0:T(8,128)S(1)}, s32[8,512]{1,0:T(8,128)S(1)}, bf16[32,2560]{1,0:T(8,128)(2,1)S(1)}, ...), condition=%wide.region_3.4_spmd.clone, body=%wide.region_2.3_spmd.clone.sunk | while | flops 357007360 | bytes 3514971 | solution.py:83
  110.1 27.5 %while.48 = (s32[]{:T(128)}, f32[32,2560]{1,0:T(8,128)S(1)}, s32[8,512]{1,0:T(8,128)S(1)}, bf16[32,2560]{1,0:T(8,128)(2,1)S(1)}, bf16[8,512,512]{2,1,0:T(8,128)(2,1)}, /*index=5*/s32[]{:T(128)}, s32[]{:T(128)}) while((s32[]{:T(128)}, f32[32,2560]{1,0:T(8,128)S(1)}, s32[8,512]{1,0:T(8,128)S(1)}, bf16[32,2560]{1,0:T(8,128)(2,1)S(1)}, ...), condition=%wide.region_5.6_spmd.clone, body=%wide.region_4.5_spmd.clone.sunk | while | flops 357007360 | bytes 3514971 | solution.py:83
  157.9 27.5 %while.49 = (s32[]{:T(128)}, f32[32,2560]{1,0:T(8,128)S(1)}, s32[8,512]{1,0:T(8,128)S(1)}, bf16[32,2560]{1,0:T(8,128)(2,1)S(1)}, bf16[8,512,512]{2,1,0:T(8,128)(2,1)}, /*index=5*/s32[]{:T(128)}, s32[]{:T(128)}) while((s32[]{:T(128)}, f32[32,2560]{1,0:T(8,128)S(1)}, s32[8,512]{1,0:T(8,128)S(1)}, bf16[32,2560]{1,0:T(8,128)(2,1)S(1)}, ...), condition=%wide.region_7.8_spmd.clone, body=%wide.region_6.7_spmd.clone.sunk | while | flops 357007360 | bytes 3514971 | solution.py:83
  205.2 29.8 %all-to-all-done = bf16[8,32,2048]{2,1,0:T(8,128)(2,1)S(1)} async-done(((bf16[8,32,2048]{2,1,0:T(8,128)(2,1)}), bf16[8,32,2048]{2,1,0:T(8,128)(2,1)S(1)}, u32[]{:S(2)}, u32[]{:S(2)}) %all-to-all-start) | async-done | bytes 1048608 | tf_op jit(solution)/shard_map/all_to_all | solution.py:106
  235.7 11.7 %cholesky.298 = f32[128,128]{1,0:T(8,128)S(1)} custom-call(f32[128,128]{1,0:T(8,128)S(1)} %cholesky.498), custom_call_target="Cholesky" | custom-call | tf_op jit(solution)/shard_map/jit(cholesky)/cholesky | solution.py:111
  247.5 9.8 %custom-call.21 = f32[1,128,128]{1,2,0:T(8,128)S(1)} custom-call(f32[1,128,128]{2,1,0:T(8,128)S(1)} %get-tuple-element.325), custom_call_target="InvertDiagBlocksLowerTriangular" | custom-call | tf_op jit(solution)/shard_map/jit(cholesky)/cholesky | solution.py:111
  257.8 11.7 %cholesky.315 = f32[128,128]{1,0:T(8,128)S(1)} custom-call(f32[128,128]{1,0:T(8,128)S(1)} %convolution_subtract_fusion.1), custom_call_target="Cholesky" | custom-call | tf_op jit(solution)/shard_map/jit(cholesky)/cholesky | solution.py:111
  281.7 11.7 %cholesky.332 = f32[128,128]{1,0:T(8,128)S(1)} custom-call(f32[128,128]{1,0:T(8,128)S(1)} %cholesky.501), custom_call_target="Cholesky" | custom-call | tf_op jit(solution)/shard_map/jit(cholesky)/cholesky | solution.py:114
  293.5 9.8 %custom-call.22 = f32[1,128,128]{1,2,0:T(8,128)S(1)} custom-call(f32[1,128,128]{2,1,0:T(8,128)S(1)} %get-tuple-element.321), custom_call_target="InvertDiagBlocksLowerTriangular" | custom-call | tf_op jit(solution)/shard_map/jit(cholesky)/cholesky | solution.py:114
  303.7 11.7 %cholesky.349 = f32[128,128]{1,0:T(8,128)S(1)} custom-call(f32[128,128]{1,0:T(8,128)S(1)} %slice_subtract_fusion.4), custom_call_target="Cholesky" | custom-call | tf_op jit(solution)/shard_map/jit(cholesky)/cholesky | solution.py:114
  324.4 11.7 %cholesky.366 = f32[128,128]{1,0:T(8,128)S(1)} custom-call(f32[128,128]{1,0:T(8,128)S(1)} %cholesky.504), custom_call_target="Cholesky" | custom-call | tf_op jit(solution)/shard_map/jit(cholesky)/cholesky | solution.py:114
  336.2 9.8 %custom-call.23 = f32[1,128,128]{1,2,0:T(8,128)S(1)} custom-call(f32[1,128,128]{2,1,0:T(8,128)S(1)} %get-tuple-element.317), custom_call_target="InvertDiagBlocksLowerTriangular" | custom-call | tf_op jit(solution)/shard_map/jit(cholesky)/cholesky | solution.py:114
  346.5 11.7 %cholesky.383 = f32[128,128]{1,0:T(8,128)S(1)} custom-call(f32[128,128]{1,0:T(8,128)S(1)} %slice_subtract_fusion.3), custom_call_target="Cholesky" | custom-call | tf_op jit(solution)/shard_map/jit(cholesky)/cholesky | solution.py:114
  368.3 11.7 %cholesky.400 = f32[128,128]{1,0:T(8,128)S(1)} custom-call(f32[128,128]{1,0:T(8,128)S(1)} %cholesky.507), custom_call_target="Cholesky" | custom-call | tf_op jit(solution)/shard_map/jit(cholesky)/cholesky | solution.py:114
  380.1 9.8 %custom-call.24 = f32[1,128,128]{1,2,0:T(8,128)S(1)} custom-call(f32[1,128,128]{2,1,0:T(8,128)S(1)} %get-tuple-element.313), custom_call_target="InvertDiagBlocksLowerTriangular" | custom-call | tf_op jit(solution)/shard_map/jit(cholesky)/cholesky | solution.py:114
  390.4 11.7 %cholesky.417 = f32[128,128]{1,0:T(8,128)S(1)} custom-call(f32[128,128]{1,0:T(8,128)S(1)} %slice_subtract_fusion.2), custom_call_target="Cholesky" | custom-call | tf_op jit(solution)/shard_map/jit(cholesky)/cholesky | solution.py:114
  410.4 11.7 %cholesky.434 = f32[128,128]{1,0:T(8,128)S(1)} custom-call(f32[128,128]{1,0:T(8,128)S(1)} %cholesky.510), custom_call_target="Cholesky" | custom-call | tf_op jit(solution)/shard_map/jit(cholesky)/cholesky | solution.py:114
  422.2 9.8 %custom-call.25 = f32[1,128,128]{1,2,0:T(8,128)S(1)} custom-call(f32[1,128,128]{2,1,0:T(8,128)S(1)} %get-tuple-element.309), custom_call_target="InvertDiagBlocksLowerTriangular" | custom-call | tf_op jit(solution)/shard_map/jit(cholesky)/cholesky | solution.py:114
  432.5 11.7 %cholesky.451 = f32[128,128]{1,0:T(8,128)S(1)} custom-call(f32[128,128]{1,0:T(8,128)S(1)} %slice_subtract_fusion.1), custom_call_target="Cholesky" | custom-call | tf_op jit(solution)/shard_map/jit(cholesky)/cholesky | solution.py:114
  454.0 11.7 %cholesky.468 = f32[128,128]{1,0:T(8,128)S(1)} custom-call(f32[128,128]{1,0:T(8,128)S(1)} %cholesky.513), custom_call_target="Cholesky" | custom-call | tf_op jit(solution)/shard_map/jit(cholesky)/cholesky | solution.py:114
  465.8 9.8 %custom-call.26 = f32[1,128,128]{1,2,0:T(8,128)S(1)} custom-call(f32[1,128,128]{2,1,0:T(8,128)S(1)} %get-tuple-element.305), custom_call_target="InvertDiagBlocksLowerTriangular" | custom-call | tf_op jit(solution)/shard_map/jit(cholesky)/cholesky | solution.py:114
  476.1 11.7 %cholesky.485 = f32[128,128]{1,0:T(8,128)S(1)} custom-call(f32[128,128]{1,0:T(8,128)S(1)} %slice_subtract_fusion), custom_call_target="Cholesky" | custom-call | tf_op jit(solution)/shard_map/jit(cholesky)/cholesky | solution.py:114
  494.9 19.7 %custom-call.11 = f32[2,128,128]{1,2,0:T(8,128)S(1)} custom-call(f32[2,128,128]{2,1,0:T(8,128)S(1)} %get-tuple-element.145), custom_call_target="InvertDiagBlocksLowerTriangular" | custom-call | tf_op jit(solution)/shard_map/triangular_solve | solution.py:46
  (309 shorter events, 263.6 us)
Async XLA Ops:
  2.5 5.6 %collective-permute-start = (bf16[32,256]{1,0:T(8,128)(2,1)S(1)}, bf16[32,256]{1,0:T(8,128)(2,1)S(1)}, u32[]{:S(2)}, u32[]{:S(2)}) collective-permute-start(bf16[32,256]{1,0:T(8,128)(2,1)S(1)} %get-tuple-element.344), channel_id=1, source_target_pairs={{0,8},{8,16},{16,24},{24,32},{32,40},{40,48},{48,56},{56,64},{64,7... | collective-permute-start | bytes 49160 | tf_op jit(solution)/shard_map/ppermute | solution.py:20
  4.4 5.1 collective-permute-start.1
  42.6 19.7 %copy-start.1 = (s32[8,512]{1,0:T(8,128)S(1)}, s32[8,512]{1,0:T(8,128)}, u32[]{:S(2)}) copy-start(s32[8,512]{1,0:T(8,128)} %get-tuple-element.648) | copy-start | bytes 49156
  42.6 7.2 %collective-permute-start.2 = (f32[32,256]{1,0:T(8,128)S(1)}, f32[32,256]{1,0:T(8,128)S(1)}, u32[]{:S(2)}, u32[]{:S(2)}) collective-permute-start(f32[32,256]{1,0:T(8,128)S(1)} %get-tuple-element.301), channel_id=1, source_target_pairs={{0,8},{8,16},{16,24},{24,32},{32,40},{40,48},{48,56},{56,64},{64,7... | collective-permute-start | bytes 98312 | tf_op jit(solution)/shard_map/ppermute | solution.py:20
  47.9 3.5 collective-permute-start.3
  53.2 7.7 %collective-permute-start.4 = (bf16[32,256]{1,0:T(8,128)(2,1)S(1)}, bf16[32,256]{1,0:T(8,128)(2,1)S(1)}, u32[]{:S(2)}, u32[]{:S(2)}) collective-permute-start(bf16[32,256]{1,0:T(8,128)(2,1)S(1)} %get-tuple-element.342), channel_id=1, source_target_pairs={{0,8},{8,16},{16,24},{24,32},{32,40},{40,48},{48,56},{56,64},{64,7... | collective-permute-start | bytes 49160 | tf_op jit(solution)/shard_map/ppermute | solution.py:20
  59.0 3.4 collective-permute-start.5
  62.4 37.7 %copy-start = (f32[32,2048]{1,0:T(8,128)S(1)}, f32[32,2048]{1,0:T(8,128)}, u32[]{:S(2)}) copy-start(f32[32,2048]{1,0:T(8,128)} %param.14) | copy-start | bytes 786436
  89.9 7.7 %collective-permute-start.6 = (f32[32,256]{1,0:T(8,128)S(1)}, f32[32,256]{1,0:T(8,128)S(1)}, u32[]{:S(2)}, u32[]{:S(2)}) collective-permute-start(f32[32,256]{1,0:T(8,128)S(1)} %get-tuple-element.299), channel_id=1, source_target_pairs={{0,8},{8,16},{16,24},{24,32},{32,40},{40,48},{48,56},{56,64},{64,7... | collective-permute-start | bytes 98312 | tf_op jit(solution)/shard_map/ppermute | solution.py:20
  95.6 3.5 collective-permute-start.7
  101.0 7.7 %collective-permute-start.8 = (bf16[32,256]{1,0:T(8,128)(2,1)S(1)}, bf16[32,256]{1,0:T(8,128)(2,1)S(1)}, u32[]{:S(2)}, u32[]{:S(2)}) collective-permute-start(bf16[32,256]{1,0:T(8,128)(2,1)S(1)} %get-tuple-element.340), channel_id=1, source_target_pairs={{0,8},{8,16},{16,24},{24,32},{32,40},{40,48},{48,56},{56,64},{64,7... | collective-permute-start | bytes 49160 | tf_op jit(solution)/shard_map/ppermute | solution.py:20
  106.8 3.4 collective-permute-start.9
  137.6 7.9 %collective-permute-start.10 = (f32[32,256]{1,0:T(8,128)S(1)}, f32[32,256]{1,0:T(8,128)S(1)}, u32[]{:S(2)}, u32[]{:S(2)}) collective-permute-start(f32[32,256]{1,0:T(8,128)S(1)} %get-tuple-element.297), channel_id=1, source_target_pairs={{0,8},{8,16},{16,24},{24,32},{32,40},{40,48},{48,56},{56,64},{64,7... | collective-permute-start | bytes 98312 | tf_op jit(solution)/shard_map/ppermute | solution.py:20
  143.4 3.5 collective-permute-start.11
  148.7 7.7 %collective-permute-start.12 = (bf16[32,256]{1,0:T(8,128)(2,1)S(1)}, bf16[32,256]{1,0:T(8,128)(2,1)S(1)}, u32[]{:S(2)}, u32[]{:S(2)}) collective-permute-start(bf16[32,256]{1,0:T(8,128)(2,1)S(1)} %get-tuple-element.338), channel_id=1, source_target_pairs={{0,8},{8,16},{16,24},{24,32},{32,40},{40,48},{48,56},{56,64},{64,7... | collective-permute-start | bytes 49160 | tf_op jit(solution)/shard_map/ppermute | solution.py:20
  154.5 3.4 collective-permute-start.13
  185.4 7.7 %collective-permute-start.14 = (f32[32,256]{1,0:T(8,128)S(1)}, f32[32,256]{1,0:T(8,128)S(1)}, u32[]{:S(2)}, u32[]{:S(2)}) collective-permute-start(f32[32,256]{1,0:T(8,128)S(1)} %get-tuple-element.295), channel_id=1, source_target_pairs={{0,8},{8,16},{16,24},{24,32},{32,40},{40,48},{48,56},{56,64},{64,7... | collective-permute-start | bytes 98312 | tf_op jit(solution)/shard_map/ppermute | solution.py:20
  191.1 3.5 collective-permute-start.15
  196.8 38.3 %all-to-all-start = ((bf16[8,32,2048]{2,1,0:T(8,128)(2,1)}), bf16[8,32,2048]{2,1,0:T(8,128)(2,1)S(1)}, u32[]{:S(2)}, u32[]{:S(2)}) async-start(bf16[8,32,2048]{2,1,0:T(8,128)(2,1)} %stack.2), calls=%async_computation | async-start | bytes 2097152 | tf_op jit(solution)/shard_map/all_to_all | solution.py:106
  271.5 9.7 %collective-permute-start.16 = (bf16[256,256]{1,0:T(8,128)(2,1)S(1)}, bf16[256,256]{1,0:T(8,128)(2,1)S(1)}, u32[]{:S(2)}, u32[]{:S(2)}) collective-permute-start(bf16[256,256]{1,0:T(8,128)(2,1)S(1)} %fusion.141), channel_id=1, source_target_pairs={{0,8},{8,0},{16,24},{24,16},{32,40},{40,32},{48,56},{56,48},{64,72... | collective-permute-start | bytes 393224 | tf_op jit(solution)/shard_map/ppermute | solution.py:32
  318.1 5.9 %collective-permute-start.17 = (bf16[256,256]{1,0:T(8,128)(2,1)S(1)}, bf16[256,256]{1,0:T(8,128)(2,1)S(1)}, u32[]{:S(2)}, u32[]{:S(2)}) collective-permute-start(bf16[256,256]{1,0:T(8,128)(2,1)S(1)} %fusion.143), channel_id=1, source_target_pairs={{0,16},{8,24},{16,0},{24,8},{32,48},{40,56},{48,32},{56,40},{64,80... | collective-permute-start | bytes 393224 | tf_op jit(solution)/shard_map/ppermute | solution.py:32
  360.9 7.0 %collective-permute-start.18 = (bf16[256,256]{1,0:T(8,128)(2,1)S(1)}, bf16[256,256]{1,0:T(8,128)(2,1)S(1)}, u32[]{:S(2)}, u32[]{:S(2)}) collective-permute-start(bf16[256,256]{1,0:T(8,128)(2,1)S(1)} %fusion.145), channel_id=1, source_target_pairs={{0,32},{8,40},{16,48},{24,56},{32,0},{40,8},{48,16},{56,24},{64,96... | collective-permute-start | bytes 393224 | tf_op jit(solution)/shard_map/ppermute | solution.py:32
  404.7 5.2 %collective-permute-start.19 = (bf16[256,256]{1,0:T(8,128)(2,1)S(1)}, bf16[256,256]{1,0:T(8,128)(2,1)S(1)}, u32[]{:S(2)}, u32[]{:S(2)}) collective-permute-start(bf16[256,256]{1,0:T(8,128)(2,1)S(1)} %fusion.147), channel_id=1, source_target_pairs={{0,64},{8,72},{16,80},{24,88},{32,96},{40,104},{48,112},{56,120},{... | collective-permute-start | bytes 393224 | tf_op jit(solution)/shard_map/ppermute | solution.py:32
  446.9 6.8 %collective-permute-start.20 = (bf16[256,256]{1,0:T(8,128)(2,1)S(1)}, bf16[256,256]{1,0:T(8,128)(2,1)S(1)}, u32[]{:S(2)}, u32[]{:S(2)}) collective-permute-start(bf16[256,256]{1,0:T(8,128)(2,1)S(1)} %fusion.149), channel_id=1, source_target_pairs={{0,128},{8,136},{16,144},{24,152},{32,160},{40,168},{48,176},{56,1... | collective-permute-start | bytes 393224 | tf_op jit(solution)/shard_map/ppermute | solution.py:32
